TPU v7x, 512 devices: a whole 4x4x16 slice. The times are simulated.
512 devices in a mesh: prow: 32 (over y, x, core), pcol: 16 (over z).
Axes of the slice: x: 4, y: 4, z: 16, core: 2. Of those that a mesh axis runs over, the one named last changes fastest.
Arguments:
- inverse_blocks: bfloat16 [128, 128, 128, 128], P('pcol', 'prow'), may hold values from -6 to 6
- lower_blocks: bfloat16 [128, 4, 128, 128], P('prow', None, 'pcol'), may hold values from -0.625 to 0.625
- pattern: int32 [4, 64], replicated, may hold values from 0 to 127, as said below
- diag_inverse: float32 [4, 16384], P(None, ('prow', 'pcol')), may hold values from -6 to 6
Outputs:
- inverse_column: float32 [128, 4, 128, 128], P('pcol', None, 'prow')
- inverse_diag: float32 [4, 16384], P(None, ('prow', 'pcol'))
Inputs may be any that keep to these rules, and one draw needn't show every extreme that they name: `pattern`: each row names 64 different ancestor blocks.
All inputs are finite; a program needn't handle non-finite values.
Results may differ from a plain program's by a relative error of at most 0.0003.
Values may be sent and summed in bfloat16 or wider, within the bound.
A program may use at most 64 MiB of HBM per device.

v0:
```python
import jax
import jax.numpy as jnp
from jax import lax
from jax.sharding import PartitionSpec as P


def broadcast(x, axis, root):
    mine = lax.axis_index(axis) == root
    return lax.psum(jnp.where(mine, x, jnp.zeros_like(x)), axis)


def per_device(inverse_blocks, lower_blocks, pattern, diag_inverse):
    blocks_i = inverse_blocks.shape[0]
    blocks_j = inverse_blocks.shape[1]
    block_width = inverse_blocks.shape[3]
    node_count = lower_blocks.shape[1]
    row_groups = lax.axis_size("prow")
    col_groups = lax.axis_size("pcol")
    block_count = blocks_j * row_groups
    ratio = row_groups // col_groups
    row_share = block_width // row_groups
    matches = pattern[None, :, :] == jnp.arange(block_count, dtype=jnp.int32)[:, None, None]
    present = jnp.sum(matches.astype(jnp.float32), axis=2)
    start_j = lax.axis_index("prow") * blocks_j
    start_i = lax.axis_index("pcol") * blocks_i
    keep_j = lax.dynamic_slice_in_dim(present, start_j, blocks_j, 0)
    keep_i = lax.dynamic_slice_in_dim(present, start_i, blocks_i, 0)
    whole = lax.all_gather(lower_blocks, "pcol", axis=2, tiled=True)
    masked = whole * keep_j.astype(jnp.bfloat16)[:, :, None, None]
    summed = lax.psum_scatter(
        jnp.einsum("ijrb,jkbe->rike", inverse_blocks, masked, preferred_element_type=jnp.float32),
        "prow",
        scatter_dimension=0,
        tiled=True,
    )
    column = summed * (-keep_i)[None, :, :, None]
    row_begin = lax.axis_index("prow") * row_share
    pieces = []
    for offset in range(ratio):
        received = broadcast(masked, "prow", lax.axis_index("pcol") * ratio + offset)
        pieces.append(lax.dynamic_slice_in_dim(received, row_begin, row_share, 2))
    own_lower = jnp.concatenate(pieces, axis=0)
    partial_value = jnp.einsum(
        "ikra,rikb->kab", own_lower.astype(jnp.float32), column, precision=lax.Precision.HIGHEST
    )
    partial_value = partial_value.reshape(node_count, block_width * block_width)
    totals = lax.psum(partial_value, ("prow", "pcol"))
    piece_len = block_width * block_width // (row_groups * col_groups)
    flat_index = lax.axis_index("prow") * col_groups + lax.axis_index("pcol")
    diag_piece = lax.dynamic_slice_in_dim(totals, flat_index * piece_len, piece_len, 1)
    return (jnp.transpose(column, (1, 2, 0, 3)), diag_inverse - diag_piece)


def solution(mesh):
    placed = (
        P("pcol", "prow", None, None),
        P("prow", None, "pcol", None),
        P(),
        P(None, ("prow", "pcol")),
    )
    return jax.shard_map(
        per_device,
        mesh=mesh,
        in_specs=placed,
        out_specs=(P("pcol", None, "prow", None), P(None, ("prow", "pcol"))),
        check_vma=False,
    )
```

profile of v0, /device:TPU:4, one launch (start us, length us, event | category | flops | bytes accessed | tf_op | source)
XLA Modules:
  0.0 766.1 jit_solution(11507525416745244874)
XLA Ops:
  7.2 0.0 copy-start
  7.2 0.0 all-reduce.6.cloned.1.call-start
  7.2 0.9 convert_reduce_fusion
  8.1 0.8 copy.15
  8.9 38.5 %all_gather.3 = bf16[4,4,128,128]{3,0,2,1:T(4,128)(2,1)S(1)} all-gather(bf16[4,4,8,128]{3,0,2,1:T(4,128)(2,1)S(1)} %copy.15), channel_id=1, replica_groups=mesh['prow'=32,'pcol'=16] {'pcol'}, dimensions={2}, use_global_device_ids=true | all-gather | bytes 557056 | tf_op jit(solution)/shard_map/all_gather | solution.py:28
  47.4 0.1 dynamic-slice_convert_fusion
  47.5 1.6 broadcast_select_fusion.1
  49.1 0.0 all-reduce.6.cloned.1.call-update
  49.2 0.0 reduce-scatter.2.cloned.1.call-start
  49.2 1.8 convolution_bitcast_fusion
  51.0 2.0 copy.17
  53.1 0.0 reduce-scatter.2.cloned.1.call-update
  53.1 0.0 all-reduce.4.cloned.1.call-start
  53.2 0.1 dynamic-slice_negate_fusion
  53.2 127.3 %all-reduce.6.cloned.1.call-done = (bf16[4,4,128,128]{3,0,2,1:T(4,128)(2,1)}, bf16[4,4,128,128]{3,0,2,1:T(4,128)(2,1)}) async-done(((bf16[4,4,128,128]{3,0,2,1:T(4,128)(2,1)}, bf16[4,4,128,128]{3,0,2,1:T(4,128)(2,1)}), (bf16[4,4,128,128]{3,0,2,1:T(4,128)(2,1)}, bf16[4,4,128,128]{3,0,2,1:T(4,128)(2,1)})) %all-reduce.6.cloned.1.call-update) | async-done | bytes 1048592 | tf_op jit(solution)/shard_map/psum | solution.py:9
  180.5 0.7 constant_dynamic-slice_fusion
  181.2 105.8 %reduce-scatter.2.cloned.1.call-done = f32[4,8,4,128]{3,1,2,0:T(8,128)} async-done(((f32[128,8,4,128]{3,1,2,0:T(8,128)}), f32[4,8,4,128]{3,1,2,0:T(8,128)}) %reduce-scatter.2.cloned.1.call-update) | async-done | bytes 65552 | tf_op jit(solution)/shard_map/reduce_scatter | solution.py:30
  287.1 1.2 convolution_bitcast_fusion.1
  288.2 0.9 copy.31
  289.1 0.0 all-reduce.4.cloned.1.call-update
  289.1 0.9 fusion.7
  290.0 0.7 copy.19
  290.7 467.6 %all-reduce.4.cloned.1.call-done = f32[4,16384]{1,0:T(4,128)} async-done(((f32[4,16384]{1,0:T(4,128)}), f32[4,16384]{1,0:T(4,128)}) %all-reduce.4.cloned.1.call-update) | async-done | bytes 262160 | tf_op jit(solution)/shard_map/psum | solution.py:47
  758.3 1.3 dynamic-slice_subtract_fusion
  (3 shorter events, 0.0 us)
Async XLA Ops:
  7.2 42.1 %copy-start = (bf16[8,4,128,128]{3,2,1,0:T(8,128)(2,1)S(1)}, bf16[8,4,128,128]{3,2,1,0:T(8,128)(2,1)}, u32[]{:S(2)}) copy-start(bf16[8,4,128,128]{3,2,1,0:T(8,128)(2,1)} %param.4) | copy-start | bytes 3145732
  7.2 173.3 %all-reduce.6.cloned.1.call-start = ((), (), s32[]{:S(2)}) async-start(), calls=%async_computation.3 | async-start | bytes 2097152 | tf_op jit(solution)/shard_map/psum | solution.py:9
  49.2 237.9 %reduce-scatter.2.cloned.1.call-start = ((), (), s32[]{:S(2)}) async-start(), calls=%async_computation.1 | async-start | bytes 2162688 | tf_op jit(solution)/shard_map/reduce_scatter | solution.py:30
  53.1 705.2 %copy-start.1 = (f32[4,32]{1,0:T(4,128)S(1)}, f32[4,32]{1,0:T(4,128)}, u32[]{:S(2)}) copy-start(f32[4,32]{1,0:T(4,128)} %param.7) | copy-start | bytes 1540
  53.1 705.2 %all-reduce.4.cloned.1.call-start = ((), (), s32[]{:S(2)}) async-start(), calls=%async_computation.2 | async-start | bytes 524288 | tf_op jit(solution)/shard_map/psum | solution.py:47
Sparse Core Ops, SparseCore 0:
  49.3 131.1 all-reduce.5
  184.9 102.0 reduce-scatter.1
  292.5 465.7 all-reduce.3
where the time goes:
time: 767 us; the launch traced here: 766 us
  waiting for transfers between devices  701 us (91%)
  blocking collectives  38.5 us (5%)
  between operations  13.8 us (2%)
    psum x1, waiting for transfers between devices, per_device(): totals = lax.psum(partial_value, ('prow', 'pcol'))  468 us
    psum x1, waiting for transfers between devices, broadcast(): return lax.psum(jnp.where(mine, x, jnp.zeros_like(x)), axis)  127 us
    reduce_scatter x1, waiting for transfers between devices, per_device(): lax.psum_scatter(jnp.einsum('ijrb,jkbe->rike', inverse_blocks, masked, pr...  106 us
    all_gather x1, blocking collectives, per_device(): whole = lax.all_gather(lower_blocks, 'pcol', axis=2, tiled=True)  38.5 us
  transfers between devices with their start and end apart: 3, of which 3 were waited for; matrix products, arithmetic and copies ran while one was open for 1% of the time, Pallas kernels for 0%

commit v1 on v0

--- a/solution.py
+++ b/solution.py
@@ -44,7 +44,7 @@
         "ikra,rikb->kab", own_lower.astype(jnp.float32), column, precision=lax.Precision.HIGHEST
     )
     partial_value = partial_value.reshape(node_count, block_width * block_width)
-    totals = lax.psum(partial_value, ("prow", "pcol"))
+    totals = lax.psum(lax.psum(partial_value, "pcol"), "prow")
     piece_len = block_width * block_width // (row_groups * col_groups)
     flat_index = lax.axis_index("prow") * col_groups + lax.axis_index("pcol")
     diag_piece = lax.dynamic_slice_in_dim(totals, flat_index * piece_len, piece_len, 1)

time: 767 us -> 568 us (0.74)
  the two profiles are of different devices: /device:TPU:4 before, /device:TPU:1 now
where the time goes in v1:
time: 568 us
  waiting for transfers between devices  509 us (90%)
  blocking collectives  31.8 us (6%)
  between operations  13.8 us (2%)
    psum x2, waiting for transfers between devices, per_device(): totals = lax.psum(lax.psum(partial_value, 'pcol'), 'prow')  270 us
    psum x1, waiting for transfers between devices, broadcast(): return lax.psum(jnp.where(mine, x, jnp.zeros_like(x)), axis)  135 us
    reduce_scatter x1, waiting for transfers between devices, per_device(): lax.psum_scatter(jnp.einsum('ijrb,jkbe->rike', inverse_blocks, masked, pr...  104 us
    all_gather x1, blocking collectives, per_device(): whole = lax.all_gather(lower_blocks, 'pcol', axis=2, tiled=True)  31.8 us
  transfers between devices with their start and end apart: 4, of which 4 were waited for; matrix products, arithmetic and copies ran while one was open for 1% of the time, Pallas kernels for 0%

profile of v1, /device:TPU:1, one launch (start us, length us, event | category | flops | bytes accessed | tf_op | source)
XLA Modules:
  0.0 567.6 jit_solution(17284687112234744055)
XLA Ops:
  7.2 0.0 all-reduce.9.cloned.1.call-start
  7.2 0.9 convert_reduce_fusion
  8.1 0.8 copy.15
  8.9 31.8 %all_gather.3 = bf16[4,4,128,128]{3,0,2,1:T(4,128)(2,1)S(1)} all-gather(bf16[4,4,8,128]{3,0,2,1:T(4,128)(2,1)S(1)} %copy.15), channel_id=1, replica_groups=mesh['prow'=32,'pcol'=16] {'pcol'}, dimensions={2}, use_global_device_ids=true | all-gather | bytes 557056 | tf_op jit(solution)/shard_map/all_gather | solution.py:28
  40.7 0.1 dynamic-slice_convert_fusion
  40.8 1.6 broadcast_select_fusion.1
  42.4 0.0 all-reduce.9.cloned.1.call-update
  42.4 0.0 reduce-scatter.2.cloned.1.call-start
  42.5 1.8 convolution_bitcast_fusion
  44.3 2.0 copy.17
  46.3 0.0 reduce-scatter.2.cloned.1.call-update
  46.4 0.0 all-reduce.5.cloned.1.call-start
  46.4 0.1 dynamic-slice_negate_fusion
  46.5 135.4 %all-reduce.9.cloned.1.call-done = (bf16[4,4,128,128]{3,0,2,1:T(4,128)(2,1)}, bf16[4,4,128,128]{3,0,2,1:T(4,128)(2,1)}) async-done(((bf16[4,4,128,128]{3,0,2,1:T(4,128)(2,1)}, bf16[4,4,128,128]{3,0,2,1:T(4,128)(2,1)}), (bf16[4,4,128,128]{3,0,2,1:T(4,128)(2,1)}, bf16[4,4,128,128]{3,0,2,1:T(4,128)(2,1)})) %all-reduce.9.cloned.1.call-update) | async-done | bytes 1048592 | tf_op jit(solution)/shard_map/psum | solution.py:9
  181.9 0.7 constant_dynamic-slice_fusion
  182.6 103.9 %reduce-scatter.2.cloned.1.call-done = f32[4,8,4,128]{3,1,2,0:T(8,128)} async-done(((f32[128,8,4,128]{3,1,2,0:T(8,128)}), f32[4,8,4,128]{3,1,2,0:T(8,128)}) %reduce-scatter.2.cloned.1.call-update) | async-done | bytes 65552 | tf_op jit(solution)/shard_map/reduce_scatter | solution.py:30
  286.5 1.2 convolution_bitcast_fusion.1
  287.7 0.9 copy.31
  288.6 0.0 all-reduce.7.cloned.1.call-start
  288.7 128.8 %all-reduce.5.cloned.1.call-done = f32[4,16384]{1,0:T(4,128)} async-done(((f32[4,16384]{1,0:T(4,128)}), f32[4,16384]{1,0:T(4,128)}) %all-reduce.5.cloned.1.call-update) | async-done | bytes 262160 | tf_op jit(solution)/shard_map/psum | solution.py:47
  417.5 0.9 fusion.7
  418.4 0.7 copy.19
  419.1 140.7 %all-reduce.7.cloned.1.call-done = f32[4,16384]{1,0:T(4,128)} async-done(((f32[4,16384]{1,0:T(4,128)}), f32[4,16384]{1,0:T(4,128)}) %all-reduce.7.cloned.1.call-update) | async-done | bytes 262160 | tf_op jit(solution)/shard_map/psum | solution.py:47
  559.8 1.3 dynamic-slice_subtract_fusion
  (6 shorter events, 0.0 us)
Async XLA Ops:
  7.2 35.3 %copy-start = (bf16[8,4,128,128]{3,2,1,0:T(8,128)(2,1)S(1)}, bf16[8,4,128,128]{3,2,1,0:T(8,128)(2,1)}, u32[]{:S(2)}) copy-start(bf16[8,4,128,128]{3,2,1,0:T(8,128)(2,1)} %param.4) | copy-start | bytes 3145732
  7.2 174.7 %all-reduce.9.cloned.1.call-start = ((), (), s32[]{:S(2)}) async-start(), calls=%async_computation.4 | async-start | bytes 2097152 | tf_op jit(solution)/shard_map/psum | solution.py:9
  42.4 244.1 %reduce-scatter.2.cloned.1.call-start = ((), (), s32[]{:S(2)}) async-start(), calls=%async_computation.1 | async-start | bytes 2162688 | tf_op jit(solution)/shard_map/reduce_scatter | solution.py:30
  46.3 513.5 %copy-start.1 = (f32[4,32]{1,0:T(4,128)S(1)}, f32[4,32]{1,0:T(4,128)}, u32[]{:S(2)}) copy-start(f32[4,32]{1,0:T(4,128)} %param.7) | copy-start | bytes 1540
  46.4 371.1 %all-reduce.5.cloned.1.call-start = ((), (), s32[]{:S(2)}) async-start(), calls=%async_computation.2 | async-start | bytes 524288 | tf_op jit(solution)/shard_map/psum | solution.py:47
  288.6 271.2 %all-reduce.7.cloned.1.call-start = ((), (), s32[]{:S(2)}) async-start(), calls=%async_computation.3 | async-start | bytes 524288 | tf_op jit(solution)/shard_map/psum | solution.py:47
Sparse Core Ops, SparseCore 0:
  42.5 139.2 all-reduce.8
  186.3 100.2 reduce-scatter.1
  288.9 128.5 all-reduce.4
  420.6 139.1 all-reduce.6

commit v2 on v0

--- a/solution.py
+++ b/solution.py
@@ -6,7 +6,7 @@
 
 def broadcast(x, axis, root):
     mine = lax.axis_index(axis) == root
-    return lax.psum(jnp.where(mine, x, jnp.zeros_like(x)), axis)
+    return jnp.sum(lax.all_gather(jnp.where(mine, x, jnp.zeros_like(x)), axis), axis=0)
 
 
 def per_device(inverse_blocks, lower_blocks, pattern, diag_inverse):

time: 767 us -> 808 us (1.053)
  waiting for transfers between devices: 701 us -> 726 us
  other arithmetic: 4.83 us -> 22.3 us
    all_gather x0 -> x2, waiting for transfers between devices: none -> 161 us  [broadcast(): lax.all_gather(jnp.where(mine, x, jnp.zeros_like(x)), axis)]
    psum x1 -> x0, waiting for transfers between devices: 127 us -> none  [broadcast(): return lax.psum(jnp.where(mine, x, jnp.zeros_like(x)), axis)]
    reduce_sum x0 -> x2, other arithmetic: none -> 17.8 us  [broadcast(): jnp.sum(lax.all_gather(jnp.where(mine, x, jnp.zeros_like(x)), axis), axis=0)]
    reduce_scatter x1, waiting for transfers between devices: 106 us -> 96.8 us  [per_device(): lax.psum_scatter(jnp.einsum('ijrb,jkbe->rike', inverse_blocks, masked, pr...]
  transfers between devices with their start and end apart: 3 -> 4, of which waited for: 3 -> 4; matrix products, arithmetic and copies ran while one was open for 1% -> 3% of each run, Pallas kernels for 0% -> 0%
where the time goes in v2:
time: 808 us
  waiting for transfers between devices  726 us (90%)
  blocking collectives  38.9 us (5%)
  other arithmetic  22.3 us (3%)
  between operations  13.8 us (2%)
    psum x1, waiting for transfers between devices, per_device(): totals = lax.psum(partial_value, ('prow', 'pcol'))  467 us
    all_gather x2, waiting for transfers between devices, broadcast(): lax.all_gather(jnp.where(mine, x, jnp.zeros_like(x)), axis)  161 us
    reduce_scatter x1, waiting for transfers between devices, per_device(): lax.psum_scatter(jnp.einsum('ijrb,jkbe->rike', inverse_blocks, masked, pr...  96.8 us
    all_gather x1, blocking collectives, per_device(): whole = lax.all_gather(lower_blocks, 'pcol', axis=2, tiled=True)  38.9 us
    reduce_sum x2, other arithmetic, broadcast(): jnp.sum(lax.all_gather(jnp.where(mine, x, jnp.zeros_like(x)), axis), axis=0)  17.8 us
  transfers between devices with their start and end apart: 4, of which 4 were waited for; matrix products, arithmetic and copies ran while one was open for 3% of the time, Pallas kernels for 0%

profile of v2, /device:TPU:4, one launch (start us, length us, event | category | flops | bytes accessed | tf_op | source)
XLA Modules:
  0.0 807.6 jit_solution(3840191016342644570)
XLA Ops:
  7.2 0.0 all-gather.7.cloned.1.call-start
  7.2 38.9 %all_gather.15 = bf16[4,4,128,128]{3,2,1,0:T(8,128)(2,1)S(1)} all-gather(bf16[4,4,8,128]{3,2,1,0:T(8,128)(2,1)} %param.5), channel_id=1, replica_groups=mesh['prow'=32,'pcol'=16] {'pcol'}, dimensions={2}, use_global_device_ids=true | all-gather | bytes 557056 | tf_op jit(solution)/shard_map/all_gather | solution.py:28
  46.2 0.8 convert_reduce_fusion
  47.0 0.1 dynamic-slice_convert_fusion
  47.0 0.1 copy.17
  47.1 1.4 broadcast_select_fusion.1
  48.6 0.0 all-gather.5.cloned.1.call-start
  48.6 0.7 all-gather.5.cloned.1.call-update
  49.3 0.0 reduce-scatter.2.cloned.1.call-start
  49.4 1.8 convolution_bitcast_fusion
  51.2 2.0 copy.19
  53.3 0.0 all-reduce.2.cloned.1.call-start
  53.3 0.1 dynamic-slice_negate_fusion
  53.4 78.9 %all-gather.7.cloned.1.call-done = bf16[128,4,128,128]{3,2,1,0:T(8,128)(2,1)} async-done(((bf16[4,4,128,128]{3,2,1,0:T(8,128)(2,1)}), bf16[128,4,128,128]{3,2,1,0:T(8,128)(2,1)}) %all-gather.7.cloned.1.call-update) | async-done | bytes 16777232 | tf_op jit(solution)/shard_map/all_gather | solution.py:9
  132.3 8.9 %reduce_sum.35 = bf16[4,4,128,128]{3,2,1,0:T(8,128)(2,1)S(1)} reduce(bf16[32,4,4,128,128]{4,3,2,1,0:T(8,128)(2,1)} %bitcast.21, bf16[]{:T(256)} %constant.28.clone.1), dimensions={0}, to_apply=%region_3.4 | reduce | flops 8126464 | bytes 17301506 | tf_op jit(solution)/shard_map/reduce_sum | solution.py:9
  141.1 81.7 %all-gather.5.cloned.1.call-done = bf16[128,4,128,128]{3,2,1,0:T(8,128)(2,1)} async-done(((bf16[4,4,128,128]{3,2,1,0:T(8,128)(2,1)}), bf16[128,4,128,128]{3,2,1,0:T(8,128)(2,1)}) %all-gather.5.cloned.1.call-update) | async-done | bytes 16777232 | tf_op jit(solution)/shard_map/all_gather | solution.py:9
  222.9 8.9 %reduce_sum.34 = bf16[4,4,128,128]{3,2,1,0:T(8,128)(2,1)S(1)} reduce(bf16[32,4,4,128,128]{4,3,2,1,0:T(8,128)(2,1)} %bitcast.22, bf16[]{:T(256)} %constant.28.clone.1), dimensions={0}, to_apply=%region_2.3 | reduce | flops 8126464 | bytes 17301506 | tf_op jit(solution)/shard_map/reduce_sum | solution.py:9
  231.8 96.8 %reduce-scatter.2.cloned.1.call-done = f32[4,8,4,128]{3,1,2,0:T(8,128)} async-done(((f32[128,8,4,128]{3,1,2,0:T(8,128)}), f32[4,8,4,128]{3,1,2,0:T(8,128)}) %reduce-scatter.2.cloned.1.call-update) | async-done | bytes 65552 | tf_op jit(solution)/shard_map/reduce_scatter | solution.py:30
  328.7 1.2 convolution_bitcast_fusion.1
  329.9 0.9 copy.37
  330.8 0.9 fusion.7
  331.7 0.7 copy.23
  332.3 467.4 %all-reduce.2.cloned.1.call-done = f32[4,16384]{1,0:T(4,128)} async-done(((f32[4,16384]{1,0:T(4,128)}), f32[4,16384]{1,0:T(4,128)}) %all-reduce.2.cloned.1.call-update) | async-done | bytes 262160 | tf_op jit(solution)/shard_map/psum | solution.py:47
  799.7 1.3 dynamic-slice_subtract_fusion
  (10 shorter events, 0.1 us)
Async XLA Ops:
  7.2 42.2 %copy-start = (bf16[8,4,128,128]{3,2,1,0:T(8,128)(2,1)S(1)}, bf16[8,4,128,128]{3,2,1,0:T(8,128)(2,1)}, u32[]{:S(2)}) copy-start(bf16[8,4,128,128]{3,2,1,0:T(8,128)(2,1)} %param.4) | copy-start | bytes 3145732
  7.2 125.1 %all-gather.7.cloned.1.call-start = ((), (), s32[]{:S(2)}) async-start(), calls=%async_computation.4 | async-start | bytes 17301504 | tf_op jit(solution)/shard_map/all_gather | solution.py:9
  48.6 174.3 %all-gather.5.cloned.1.call-start = ((), (), s32[]{:S(2)}) async-start(), calls=%async_computation.3 | async-start | bytes 17301504 | tf_op jit(solution)/shard_map/all_gather | solution.py:9
  49.3 279.4 %reduce-scatter.2.cloned.1.call-start = ((), (), s32[]{:S(2)}) async-start(), calls=%async_computation.1 | async-start | bytes 2162688 | tf_op jit(solution)/shard_map/reduce_scatter | solution.py:30
  53.3 746.5 %all-reduce.2.cloned.1.call-start = ((), (), s32[]{:S(2)}) async-start(), calls=%async_computation.2 | async-start | bytes 524288 | tf_op jit(solution)/shard_map/psum | solution.py:47
  222.9 576.8 %copy-start.1 = (f32[4,32]{1,0:T(4,128)S(1)}, f32[4,32]{1,0:T(4,128)}, u32[]{:S(2)}) copy-start(f32[4,32]{1,0:T(4,128)} %param.7) | copy-start | bytes 1540
Sparse Core Ops, SparseCore 0:
  48.7 83.5 all-gather.6
  135.4 87.4 all-gather.4
  227.3 101.3 reduce-scatter.1
  334.0 465.6 all-reduce.1
